TPU v7x, 128 devices: a whole 4x4x4 slice. The times are simulated.
128 devices in a mesh: row: 8 (over z, x_lo), col: 16 (over x_hi, y, core).
Axes of the slice: x: 4 (x_hi: 2, x_lo: 2; x = x_hi * 2 + x_lo), y: 4, z: 4, core: 2. Of those that a mesh axis runs over, the one named last changes fastest.
Arguments:
- stream: float32 [16384, 256], P(('row', 'col')), may hold values from -130 to 130
- stream_tail: float32 [31, 256], replicated, may hold values from -130 to 130
- archive: float32 [65536, 256], P(('col', 'row')), may hold values from -60 to 60
- archive_tail: float32 [31, 256], replicated, may hold values from -60 to 60
Outputs:
- row_profile: float32 [16384], P(('row', 'col'))
- col_profile: float32 [65536], P(('col', 'row'))
All inputs are finite; a program needn't handle non-finite values.
Results may differ from a plain program's by a relative error of at most 0.0003.
Values sent between devices are 32-bit elements; how exact they have to be, the bound alone decides.
A program may use at most 128 MiB of HBM per device.

v0:
```python
import jax
import jax.numpy as jnp
from jax import lax
from jax.sharding import PartitionSpec as P

M = 32


def from_behind(block, axis, distance):
    devices = range(lax.axis_size(axis))
    route = [((i - distance) % len(devices), i) for i in devices]
    return lax.ppermute(block, axis, route)


def shifted(value, axis, steps):
    count = lax.axis_size(axis)
    leading, last = (max(0, -steps), min(count, count - steps))
    return lax.ppermute(value, axis, [(source, source + steps) for source in range(leading, last)])


def to_unit(frames):
    return frames / jnp.sqrt(jnp.sum(frames * frames, axis=1, keepdims=True) + 1e-06)


def window_sum(gram_block):
    summed = gram_block
    width = 1
    while width < M:
        height = summed.shape[0] - width
        breadth = summed.shape[1] - width
        summed = summed[0:height, 0:breadth] + summed[width:, width:]
        width = width * 2
    return summed


def profile_tile(stream_ext, archive_ext):
    row_count = stream_ext.shape[0] - (M - 1)
    col_count = archive_ext.shape[0] - (M - 1)
    block_rows = min(256, row_count)
    while block_rows * col_count < 2**20 and row_count % (block_rows * 2) == 0:
        block_rows = block_rows * 2
    steps_count = row_count // block_rows

    def advance(col_best, position):
        first_row = position * block_rows
        window_rows = lax.dynamic_slice_in_dim(stream_ext, first_row, block_rows + M - 1, 0)
        gram_block = lax.dot_general(
            window_rows,
            archive_ext,
            (((1,), (1,)), ((), ())),
            precision=lax.Precision.HIGHEST,
            preferred_element_type=jnp.float32,
        )
        scores = window_sum(gram_block) / M
        return (jnp.maximum(col_best, jnp.max(scores, axis=0)), jnp.max(scores, axis=1))

    start_best = jnp.full((col_count,), -2.0, jnp.float32)
    col_best, row_best = lax.scan(advance, start_best, jnp.arange(steps_count, dtype=jnp.int32))
    return (row_best.reshape(-1), col_best)


def on_device(stream, stream_tail, archive, archive_tail):
    stream_unit = to_unit(stream)
    archive_unit = to_unit(archive)
    stream_after = to_unit(stream_tail)
    archive_after = to_unit(archive_tail)
    last_row = lax.axis_index("row") == lax.axis_size("row") - 1
    last_col = lax.axis_index("col") == lax.axis_size("col") - 1
    stream_all = lax.all_gather(stream_unit, ("row", "col"), axis=0, tiled=True)
    stream_ext = jnp.concatenate([stream_all, stream_after], axis=0)
    head_rows = archive_unit[: M - 1]
    from_below = from_behind(head_rows, "row", -1)
    from_beside = shifted(from_below, "col", -1)
    following = jnp.where(last_row, jnp.where(last_col, archive_after, from_beside), from_below)
    archive_ext = jnp.concatenate([archive_unit, following], axis=0)
    row_best, col_profile = profile_tile(stream_ext, archive_ext)
    row_best = lax.pmax(row_best, ("row", "col"))
    own_len = stream.shape[0]
    flat_index = lax.axis_index("row") * lax.axis_size("col") + lax.axis_index("col")
    row_profile = lax.dynamic_slice_in_dim(row_best, flat_index * own_len, own_len)
    return (row_profile, col_profile)


def solution(mesh):
    return jax.shard_map(
        on_device,
        mesh=mesh,
        in_specs=(P(("row", "col"), None), P(), P(("col", "row"), None), P()),
        out_specs=(P(("row", "col")), P(("col", "row"))),
        check_vma=False,
    )
```

profile of v0, /device:TPU:1, one launch (start us, length us, event | category | flops | bytes accessed | tf_op | source)
XLA Modules:
  0.0 509.9 jit_solution(15961827501369002649)
XLA Ops:
  8.2 1.6 broadcast_divide_fusion.1
  12.4 5.6 %collective-permute-start = (f32[31,256]{1,0:T(8,128)S(1)}, f32[31,256]{1,0:T(8,128)S(1)}, u32[]{:S(2)}, u32[]{:S(2)}) collective-permute-start(f32[31,256]{1,0:T(8,128)S(1)} %slice.54), channel_id=1, source_target_pairs={{16,0},{32,16},{48,32},{64,48},{80,64},{96,80},{112,96},{0,112},{1... | collective-permute-start | bytes 95240 | tf_op jit(solution)/shard_map/ppermute | solution.py:12
  20.5 2.9 collective-permute-start.1
  23.4 2.8 collective-permute-done.1
  27.1 197.7 %all-gather.2.cloned.1.call-done = f32[16384,256]{1,0:T(8,128)} async-done(((f32[128,256]{1,0:T(8,128)}), f32[16384,256]{1,0:T(8,128)}) %all-gather.2.cloned.1.call-update) | async-done | bytes 16777232 | tf_op jit(solution)/shard_map/all_gather | solution.py:69
  224.8 14.4 %pad_maximum_fusion = f32[16415,256]{1,0:T(8,128)} fusion(f32[31,256]{1,0:T(8,128)S(1)} %broadcast_divide_fusion.2, f32[16384,256]{1,0:T(8,128)} %all-gather.2.cloned.1.call-done), kind=kLoop, calls=%fused_computation.12 | loop fusion | flops 4202240 | bytes 33617920 | tf_op jit(solution)/shard_map/concatenate | solution.py:70
  239.2 123.0 %while.13 = (s32[]{:T(128)}, f32[512]{0:T(512)S(1)}, f32[8,2048]{1,0:T(8,128)S(1)}, s32[8]{0:T(128)S(1)}, f32[16415,256]{1,0:T(8,128)}, /*index=5*/f32[543,256]{...) while((s32[]{:T(128)}, f32[512]{0:T(512)S(1)}, f32[8,2048]{1,0:T(8,128)S(1)}, ...), condition=%wide.region_7.8_spmd.clone, body=%wide.region_4.7_spmd.clone.sunk | while | flops 3476612096 | bytes 68995496 | solution.py:58
  240.5 6.3 %fusion.13 = f32[2079,543]{0,1:T(8,128)S(1)} fusion(f32[543,256]{1,0:T(8,128)S(1)} %get-tuple-element.138, f32[16415,256]{1,0:T(8,128)} %get-tuple-element.137, s32[]{:T(128)S(6)} %select_n.31), kind=kOutput, calls=%fused_computation.6.clone.1 | convolution fusion | flops 3467971584 | bytes 7201544 | tf_op jit(solution)/shard_map/while/body/eval_jaxpr/dot_general | solution.py:47
  246.8 1.7 slice_add_fusion.9
  248.5 1.7 slice_add_fusion.10
  255.9 6.3 %fusion.13 = f32[2079,543]{0,1:T(8,128)S(1)} fusion(f32[543,256]{1,0:T(8,128)S(1)} %get-tuple-element.138, f32[16415,256]{1,0:T(8,128)} %get-tuple-element.137, s32[]{:T(128)S(6)} %select_n.31), kind=kOutput, calls=%fused_computation.6.clone.1 | convolution fusion | flops 3467971584 | bytes 7201544 | tf_op jit(solution)/shard_map/while/body/eval_jaxpr/dot_general | solution.py:47
  262.2 1.7 slice_add_fusion.9
  263.9 1.7 slice_add_fusion.10
  271.3 6.3 %fusion.13 = f32[2079,543]{0,1:T(8,128)S(1)} fusion(f32[543,256]{1,0:T(8,128)S(1)} %get-tuple-element.138, f32[16415,256]{1,0:T(8,128)} %get-tuple-element.137, s32[]{:T(128)S(6)} %select_n.31), kind=kOutput, calls=%fused_computation.6.clone.1 | convolution fusion | flops 3467971584 | bytes 7201544 | tf_op jit(solution)/shard_map/while/body/eval_jaxpr/dot_general | solution.py:47
  277.6 1.7 slice_add_fusion.9
  279.3 1.7 slice_add_fusion.10
  286.6 6.3 %fusion.13 = f32[2079,543]{0,1:T(8,128)S(1)} fusion(f32[543,256]{1,0:T(8,128)S(1)} %get-tuple-element.138, f32[16415,256]{1,0:T(8,128)} %get-tuple-element.137, s32[]{:T(128)S(6)} %select_n.31), kind=kOutput, calls=%fused_computation.6.clone.1 | convolution fusion | flops 3467971584 | bytes 7201544 | tf_op jit(solution)/shard_map/while/body/eval_jaxpr/dot_general | solution.py:47
  293.0 1.7 slice_add_fusion.9
  294.6 1.7 slice_add_fusion.10
  302.0 6.3 %fusion.13 = f32[2079,543]{0,1:T(8,128)S(1)} fusion(f32[543,256]{1,0:T(8,128)S(1)} %get-tuple-element.138, f32[16415,256]{1,0:T(8,128)} %get-tuple-element.137, s32[]{:T(128)S(6)} %select_n.31), kind=kOutput, calls=%fused_computation.6.clone.1 | convolution fusion | flops 3467971584 | bytes 7201544 | tf_op jit(solution)/shard_map/while/body/eval_jaxpr/dot_general | solution.py:47
  308.4 1.7 slice_add_fusion.9
  310.0 1.7 slice_add_fusion.10
  317.4 6.3 %fusion.13 = f32[2079,543]{0,1:T(8,128)S(1)} fusion(f32[543,256]{1,0:T(8,128)S(1)} %get-tuple-element.138, f32[16415,256]{1,0:T(8,128)} %get-tuple-element.137, s32[]{:T(128)S(6)} %select_n.31), kind=kOutput, calls=%fused_computation.6.clone.1 | convolution fusion | flops 3467971584 | bytes 7201544 | tf_op jit(solution)/shard_map/while/body/eval_jaxpr/dot_general | solution.py:47
  323.7 1.7 slice_add_fusion.9
  325.4 1.7 slice_add_fusion.10
  332.8 6.3 %fusion.13 = f32[2079,543]{0,1:T(8,128)S(1)} fusion(f32[543,256]{1,0:T(8,128)S(1)} %get-tuple-element.138, f32[16415,256]{1,0:T(8,128)} %get-tuple-element.137, s32[]{:T(128)S(6)} %select_n.31), kind=kOutput, calls=%fused_computation.6.clone.1 | convolution fusion | flops 3467971584 | bytes 7201544 | tf_op jit(solution)/shard_map/while/body/eval_jaxpr/dot_general | solution.py:47
  339.1 1.7 slice_add_fusion.9
  340.8 1.7 slice_add_fusion.10
  348.2 6.3 %fusion.13 = f32[2079,543]{0,1:T(8,128)S(1)} fusion(f32[543,256]{1,0:T(8,128)S(1)} %get-tuple-element.138, f32[16415,256]{1,0:T(8,128)} %get-tuple-element.137, s32[]{:T(128)S(6)} %select_n.31), kind=kOutput, calls=%fused_computation.6.clone.1 | convolution fusion | flops 3467971584 | bytes 7201544 | tf_op jit(solution)/shard_map/while/body/eval_jaxpr/dot_general | solution.py:47
  354.5 1.7 slice_add_fusion.9
  356.2 1.7 slice_add_fusion.10
  363.0 138.8 %all-reduce.2.cloned.1.call-done = f32[16384]{0:T(1024)} async-done(((f32[16384]{0:T(1024)}), f32[16384]{0:T(1024)}) %all-reduce.2.cloned.1.call-update) | async-done | bytes 65552 | tf_op jit(solution)/shard_map/pmax | solution.py:77
  (73 shorter events, 48.9 us)
Async XLA Ops:
  7.2 217.6 %all-gather.2.cloned.1.call-start = ((), (), s32[]{:S(2)}) async-start(), calls=%async_computation | async-start | bytes 16908288 | tf_op jit(solution)/shard_map/all_gather | solution.py:69
  9.9 491.9 %all-reduce.2.cloned.1.call-start = ((), (), s32[]{:S(2)}) async-start(), calls=%async_computation.1 | async-start | bytes 131072 | tf_op jit(solution)/shard_map/pmax | solution.py:77
  12.4 8.2 %collective-permute-start = (f32[31,256]{1,0:T(8,128)S(1)}, f32[31,256]{1,0:T(8,128)S(1)}, u32[]{:S(2)}, u32[]{:S(2)}) collective-permute-start(f32[31,256]{1,0:T(8,128)S(1)} %slice.54), channel_id=1, source_target_pairs={{16,0},{32,16},{48,32},{64,48},{80,64},{96,80},{112,96},{0,112},{1... | collective-permute-start | bytes 95240 | tf_op jit(solution)/shard_map/ppermute | solution.py:12
  20.5 5.7 %collective-permute-start.1 = (f32[31,256]{1,0:T(8,128)S(1)}, f32[31,256]{1,0:T(8,128)S(1)}, u32[]{:S(2)}, u32[]{:S(2)}) collective-permute-start(f32[31,256]{1,0:T(8,128)S(1)} %collective-permute-done), channel_id=1, source_target_pairs={{1,0},{2,1},{3,2},{4,3},{5,4},{6,5},{7,6},{8,7},{9,8},{10,9},{11,1... | collective-permute-start | bytes 95240 | tf_op jit(solution)/shard_map/ppermute | solution.py:18
  362.3 140.8 %copy-start = (f32[512]{0:T(512)}, f32[512]{0:T(512)S(1)}, u32[]{:S(2)}) copy-start(f32[512]{0:T(512)S(1)} %get-tuple-element.34) | copy-start | bytes 6148
Sparse Core Ops, SparseCore 0:
  10.0 214.7 all-gather.1
  363.1 138.6 all-reduce.1
where the time goes:
time: 511 us; the launch traced here: 510 us
  waiting for transfers between devices  339 us (66%)
  other arithmetic  83.3 us (16%)
  matrix products  50.6 us (10%)
  between operations  14.2 us (3%)
  starting transfers between devices  8.51 us (2%)
  local copies, waits for them, and re-layouts  8.22 us (2%)
  loops' own time  5.71 us (1%)
    all_gather x1, waiting for transfers between devices, on_device(): stream_all = lax.all_gather(stream_unit, ('row', 'col'), axis=0, tiled=True)  198 us
    pmax x1, waiting for transfers between devices, on_device(): row_best = lax.pmax(row_best, ('row', 'col'))  139 us
    dot_general x8, matrix products, advance(): lax.dot_general(window_rows, archive_ext, (((1,), (1,)), ((), ())), preci...  50.6 us
    add x32, other arithmetic, window_sum(): summed = summed[0:height, 0:breadth] + summed[width:, width:]  49.6 us
    concatenate x1, other arithmetic, on_device(): stream_ext = jnp.concatenate([stream_all, stream_after], axis=0)  14.4 us
    reduce_max x8, other arithmetic, advance(): jnp.max(scores, axis=1)  10.6 us
  transfers between devices with their start and end apart: 4, of which 3 were waited for; matrix products, arithmetic and copies ran while one was open for 1% of the time, Pallas kernels for 0%

commit v1 on v0

--- a/solution.py
+++ b/solution.py
@@ -66,7 +66,8 @@
     archive_after = to_unit(archive_tail)
     last_row = lax.axis_index("row") == lax.axis_size("row") - 1
     last_col = lax.axis_index("col") == lax.axis_size("col") - 1
-    stream_all = lax.all_gather(stream_unit, ("row", "col"), axis=0, tiled=True)
+    sent = jnp.stack([stream_unit] * lax.axis_size(("row", "col")))
+    stream_all = jnp.concatenate(lax.all_to_all(sent, ("row", "col"), 0, 0), axis=0)
     stream_ext = jnp.concatenate([stream_all, stream_after], axis=0)
     head_rows = archive_unit[: M - 1]
     from_below = from_behind(head_rows, "row", -1)

time: 511 us -> 542 us (1.061)
  waiting for transfers between devices: 339 us -> 358 us
  starting transfers between devices: 8.51 us -> 19 us
  local copies, waits for them, and re-layouts: 8.22 us -> 16 us
  other arithmetic: 83.3 us -> 77.5 us
    ppermute x1, waiting for transfers between devices: 0.01 us -> 198 us  [from_behind(): return lax.ppermute(block, axis, route)]
    all_gather x1 -> x0, waiting for transfers between devices: 198 us -> none  [on_device(): stream_all = lax.all_gather(stream_unit, ('row', 'col'), axis=0, tiled=True)]
    all_to_all x0 -> x1, starting transfers between devices: none -> 11.9 us  [on_device(): lax.all_to_all(sent, ('row', 'col'), 0, 0)]
    pmax x1, waiting for transfers between devices: 139 us -> 147 us  [on_device(): row_best = lax.pmax(row_best, ('row', 'col'))]
    another operation x0 -> x1, local copies, waits for them, and re-layouts: none -> 7.8 us  [on_device(): sent = jnp.stack([stream_unit] * lax.axis_size(('row', 'col')))]
    all_to_all x0 -> x1, waiting for transfers between devices: none -> 6.86 us  [on_device(): lax.all_to_all(sent, ('row', 'col'), 0, 0)]
  transfers between devices with their start and end apart: 4 -> 4, of which waited for: 3 -> 4; matrix products, arithmetic and copies ran while one was open for 1% -> 0% of each run, Pallas kernels for 0% -> 0%
where the time goes in v1:
time: 542 us
  waiting for transfers between devices  358 us (66%)
  other arithmetic  77.5 us (14%)
  matrix products  50.6 us (9%)
  starting transfers between devices  19 us (4%)
  local copies, waits for them, and re-layouts  16 us (3%)
  between operations  14.2 us (3%)
  loops' own time  5.71 us (1%)
    ppermute x1, waiting for transfers between devices, from_behind(): return lax.ppermute(block, axis, route)  198 us
    pmax x1, waiting for transfers between devices, on_device(): row_best = lax.pmax(row_best, ('row', 'col'))  147 us
    dot_general x8, matrix products, advance(): lax.dot_general(window_rows, archive_ext, (((1,), (1,)), ((), ())), preci...  50.6 us
    add x32, other arithmetic, window_sum(): summed = summed[0:height, 0:breadth] + summed[width:, width:]  49.6 us
    concatenate x1, other arithmetic, on_device(): stream_ext = jnp.concatenate([stream_all, stream_after], axis=0)  14.4 us
    all_to_all x1, starting transfers between devices, on_device(): lax.all_to_all(sent, ('row', 'col'), 0, 0)  11.9 us
  transfers between devices with their start and end apart: 4, of which 4 were waited for; matrix products, arithmetic and copies ran while one was open for 0% of the time, Pallas kernels for 0%

profile of v1, /device:TPU:1, one launch (start us, length us, event | category | flops | bytes accessed | tf_op | source)
XLA Modules:
  0.0 541.6 jit_solution(9242035947957610957)
XLA Ops:
  9.2 7.8 %stack.2 = f32[128,128,256]{2,1,0:T(8,128)} broadcast(f32[128,256]{1,0:T(8,128)S(1)} %broadcast_divide_fusion.1), dimensions={1,2} | broadcast | bytes 16908288 | tf_op jit(solution)/shard_map/stack | solution.py:69
  17.0 11.9 %all-to-all-start = ((f32[128,128,256]{2,1,0:T(8,128)}), f32[128,128,256]{2,1,0:T(8,128)}, u32[]{:S(2)}, u32[]{:S(2)}) async-start(f32[128,128,256]{2,1,0:T(8,128)} %stack.2), calls=%async_computation | async-start | bytes 33554432 | tf_op jit(solution)/shard_map/all_to_all | solution.py:70
  29.3 4.2 collective-permute-start
  33.9 198.2 %collective-permute-done = f32[31,256]{1,0:T(8,128)S(1)} collective-permute-done((f32[31,256]{1,0:T(8,128)S(1)}, f32[31,256]{1,0:T(8,128)S(1)}, u32[]{:S(2)}, u32[]{:S(2)}) %collective-permute-start) | collective-permute-done | bytes 31776 | tf_op jit(solution)/shard_map/ppermute | solution.py:12
  232.1 2.8 collective-permute-start.1
  234.9 6.0 %collective-permute-done.1 = f32[31,256]{1,0:T(8,128)S(1)} collective-permute-done((f32[31,256]{1,0:T(8,128)S(1)}, f32[31,256]{1,0:T(8,128)S(1)}, u32[]{:S(2)}, u32[]{:S(2)}) %collective-permute-start.1) | collective-permute-done | bytes 31776 | tf_op jit(solution)/shard_map/ppermute | solution.py:18
  241.0 6.9 %all-to-all-done = f32[128,128,256]{2,1,0:T(8,128)} async-done(((f32[128,128,256]{2,1,0:T(8,128)}), f32[128,128,256]{2,1,0:T(8,128)}, u32[]{:S(2)}, u32[]{:S(2)}) %all-to-all-start) | async-done | bytes 16777248 | tf_op jit(solution)/shard_map/all_to_all | solution.py:70
  247.9 14.4 %pad_maximum_fusion = f32[16415,256]{1,0:T(8,128)} fusion(f32[31,256]{1,0:T(8,128)S(1)} %broadcast_divide_fusion.2, f32[16384,256]{1,0:T(8,128)} %bitcast), kind=kLoop, calls=%fused_computation.12 | loop fusion | flops 4202240 | bytes 33617920 | tf_op jit(solution)/shard_map/concatenate | solution.py:71
  262.3 123.0 %while.13 = (s32[]{:T(128)}, f32[512]{0:T(512)S(1)}, f32[8,2048]{1,0:T(8,128)S(1)}, s32[8]{0:T(128)S(1)}, f32[16415,256]{1,0:T(8,128)}, /*index=5*/f32[543,256]{...) while((s32[]{:T(128)}, f32[512]{0:T(512)S(1)}, f32[8,2048]{1,0:T(8,128)S(1)}, ...), condition=%wide.region_7.8_spmd.clone, body=%wide.region_4.7_spmd.clone.sunk | while | flops 3476612096 | bytes 68995496 | solution.py:58
  263.6 6.3 %fusion.13 = f32[2079,543]{0,1:T(8,128)S(1)} fusion(f32[543,256]{1,0:T(8,128)S(1)} %get-tuple-element.138, f32[16415,256]{1,0:T(8,128)} %get-tuple-element.137, s32[]{:T(128)S(6)} %select_n.31), kind=kOutput, calls=%fused_computation.6.clone.1 | convolution fusion | flops 3467971584 | bytes 7201544 | tf_op jit(solution)/shard_map/while/body/eval_jaxpr/dot_general | solution.py:47
  269.9 1.7 slice_add_fusion.9
  271.6 1.7 slice_add_fusion.10
  279.0 6.3 %fusion.13 = f32[2079,543]{0,1:T(8,128)S(1)} fusion(f32[543,256]{1,0:T(8,128)S(1)} %get-tuple-element.138, f32[16415,256]{1,0:T(8,128)} %get-tuple-element.137, s32[]{:T(128)S(6)} %select_n.31), kind=kOutput, calls=%fused_computation.6.clone.1 | convolution fusion | flops 3467971584 | bytes 7201544 | tf_op jit(solution)/shard_map/while/body/eval_jaxpr/dot_general | solution.py:47
  285.3 1.7 slice_add_fusion.9
  287.0 1.7 slice_add_fusion.10
  294.3 6.3 %fusion.13 = f32[2079,543]{0,1:T(8,128)S(1)} fusion(f32[543,256]{1,0:T(8,128)S(1)} %get-tuple-element.138, f32[16415,256]{1,0:T(8,128)} %get-tuple-element.137, s32[]{:T(128)S(6)} %select_n.31), kind=kOutput, calls=%fused_computation.6.clone.1 | convolution fusion | flops 3467971584 | bytes 7201544 | tf_op jit(solution)/shard_map/while/body/eval_jaxpr/dot_general | solution.py:47
  300.7 1.7 slice_add_fusion.9
  302.4 1.7 slice_add_fusion.10
  309.7 6.3 %fusion.13 = f32[2079,543]{0,1:T(8,128)S(1)} fusion(f32[543,256]{1,0:T(8,128)S(1)} %get-tuple-element.138, f32[16415,256]{1,0:T(8,128)} %get-tuple-element.137, s32[]{:T(128)S(6)} %select_n.31), kind=kOutput, calls=%fused_computation.6.clone.1 | convolution fusion | flops 3467971584 | bytes 7201544 | tf_op jit(solution)/shard_map/while/body/eval_jaxpr/dot_general | solution.py:47
  316.1 1.7 slice_add_fusion.9
  317.7 1.7 slice_add_fusion.10
  325.1 6.3 %fusion.13 = f32[2079,543]{0,1:T(8,128)S(1)} fusion(f32[543,256]{1,0:T(8,128)S(1)} %get-tuple-element.138, f32[16415,256]{1,0:T(8,128)} %get-tuple-element.137, s32[]{:T(128)S(6)} %select_n.31), kind=kOutput, calls=%fused_computation.6.clone.1 | convolution fusion | flops 3467971584 | bytes 7201544 | tf_op jit(solution)/shard_map/while/body/eval_jaxpr/dot_general | solution.py:47
  331.4 1.7 slice_add_fusion.9
  333.1 1.7 slice_add_fusion.10
  340.5 6.3 %fusion.13 = f32[2079,543]{0,1:T(8,128)S(1)} fusion(f32[543,256]{1,0:T(8,128)S(1)} %get-tuple-element.138, f32[16415,256]{1,0:T(8,128)} %get-tuple-element.137, s32[]{:T(128)S(6)} %select_n.31), kind=kOutput, calls=%fused_computation.6.clone.1 | convolution fusion | flops 3467971584 | bytes 7201544 | tf_op jit(solution)/shard_map/while/body/eval_jaxpr/dot_general | solution.py:47
  346.8 1.7 slice_add_fusion.9
  348.5 1.7 slice_add_fusion.10
  355.9 6.3 %fusion.13 = f32[2079,543]{0,1:T(8,128)S(1)} fusion(f32[543,256]{1,0:T(8,128)S(1)} %get-tuple-element.138, f32[16415,256]{1,0:T(8,128)} %get-tuple-element.137, s32[]{:T(128)S(6)} %select_n.31), kind=kOutput, calls=%fused_computation.6.clone.1 | convolution fusion | flops 3467971584 | bytes 7201544 | tf_op jit(solution)/shard_map/while/body/eval_jaxpr/dot_general | solution.py:47
  362.2 1.7 slice_add_fusion.9
  371.3 6.3 %fusion.13 = f32[2079,543]{0,1:T(8,128)S(1)} fusion(f32[543,256]{1,0:T(8,128)S(1)} %get-tuple-element.138, f32[16415,256]{1,0:T(8,128)} %get-tuple-element.137, s32[]{:T(128)S(6)} %select_n.31), kind=kOutput, calls=%fused_computation.6.clone.1 | convolution fusion | flops 3467971584 | bytes 7201544 | tf_op jit(solution)/shard_map/while/body/eval_jaxpr/dot_general | solution.py:47
  379.3 1.7 slice_add_fusion.10
  386.1 147.4 %all-reduce.2.cloned.1.call-done = f32[16384]{0:T(1024)} async-done(((f32[16384]{0:T(1024)}), f32[16384]{0:T(1024)}) %all-reduce.2.cloned.1.call-update) | async-done | bytes 65552 | tf_op jit(solution)/shard_map/pmax | solution.py:78
  (79 shorter events, 48.0 us)
Async XLA Ops:
  17.0 12.0 %copy-start = (f32[512,256]{1,0:T(8,128)S(1)}, f32[512,256]{1,0:T(8,128)}, u32[]{:S(2)}) copy-start(f32[512,256]{1,0:T(8,128)} %param.8) | copy-start | bytes 1572868
  17.0 16.6 %copy-start.1 = (f32[31,256]{1,0:T(8,128)S(1)}, f32[31,256]{1,0:T(8,128)}, u32[]{:S(2)}) copy-start(f32[31,256]{1,0:T(8,128)} %param.7) | copy-start | bytes 95236
  17.0 16.8 %copy-start.2 = (f32[31,256]{1,0:T(8,128)S(1)}, f32[31,256]{1,0:T(8,128)}, u32[]{:S(2)}) copy-start(f32[31,256]{1,0:T(8,128)} %param.9) | copy-start | bytes 95236
  17.0 230.9 %all-to-all-start = ((f32[128,128,256]{2,1,0:T(8,128)}), f32[128,128,256]{2,1,0:T(8,128)}, u32[]{:S(2)}, u32[]{:S(2)}) async-start(f32[128,128,256]{2,1,0:T(8,128)} %stack.2), calls=%async_computation | async-start | bytes 33554432 | tf_op jit(solution)/shard_map/all_to_all | solution.py:70
  29.0 504.5 %all-reduce.2.cloned.1.call-start = ((), (), s32[]{:S(2)}) async-start(), calls=%async_computation.1 | async-start | bytes 131072 | tf_op jit(solution)/shard_map/pmax | solution.py:78
  29.3 202.7 %collective-permute-start = (f32[31,256]{1,0:T(8,128)S(1)}, f32[31,256]{1,0:T(8,128)S(1)}, u32[]{:S(2)}, u32[]{:S(2)}) collective-permute-start(f32[31,256]{1,0:T(8,128)S(1)} %slice.54), channel_id=1, source_target_pairs={{16,0},{32,16},{48,32},{64,48},{80,64},{96,80},{112,96},{0,112},{1... | collective-permute-start | bytes 95240 | tf_op jit(solution)/shard_map/ppermute | solution.py:12
  232.1 8.8 %collective-permute-start.1 = (f32[31,256]{1,0:T(8,128)S(1)}, f32[31,256]{1,0:T(8,128)S(1)}, u32[]{:S(2)}, u32[]{:S(2)}) collective-permute-start(f32[31,256]{1,0:T(8,128)S(1)} %collective-permute-done), channel_id=1, source_target_pairs={{1,0},{2,1},{3,2},{4,3},{5,4},{6,5},{7,6},{8,7},{9,8},{10,9},{11,1... | collective-permute-start | bytes 95240 | tf_op jit(solution)/shard_map/ppermute | solution.py:18
  385.4 149.4 %copy-start.3 = (f32[512]{0:T(512)}, f32[512]{0:T(512)S(1)}, u32[]{:S(2)}) copy-start(f32[512]{0:T(512)S(1)} %get-tuple-element.34) | copy-start | bytes 6148
Sparse Core Ops, SparseCore 0:
  386.2 147.2 all-reduce.1
